TPU v7x, 32 devices: a whole 2x2x4 slice. The times are simulated.
32 devices in a mesh: groups: 2 (over y), st: 4 (over x, core), ch: 4 (over z).
Axes of the slice: x: 2, y: 2, z: 4, core: 2. Of those that a mesh axis runs over, the one named last changes fastest.
Arguments:
- latents: bfloat16 [1280, 1024], P('ch', ('groups', 'st')), parts along dimension 1, may hold values from -6 to 6
- spatial_weight: bfloat16 [9, 1280, 1280], P(None, 'ch'), may hold values from -0.0546875 to 0.0546875
- temporal_weight: bfloat16 [3, 1280, 1280], P(None, 'ch'), may hold values from -0.09375 to 0.09375
- cotangent: bfloat16 [1280, 1024], P('ch', ('groups', 'st')), parts along dimension 1, may hold values from -6 to 6
Outputs:
- temporal_out: bfloat16 [1280, 1024], P('ch', ('groups', 'st')), parts along dimension 1
- latent_grad: bfloat16 [1280, 1024], P('ch', ('groups', 'st')), parts along dimension 1
- spatial_grad: float32 [18, 1280, 1280], P('groups', 'ch', 'st'), parts along dimension 0
- temporal_grad: float32 [6, 1280, 1280], P('groups', 'ch', 'st'), parts along dimension 0
There are 2 independent parts, one for each index of `groups`. A program takes and returns all parts, laid end to end along the dimension named above; an argument that names none is the same for every part. Nothing has to cross between parts.
All inputs are finite; a program needn't handle non-finite values.
Results may differ from a plain program's by a relative error of at most 0.008.
Values may be sent and summed in bfloat16 or wider, within the bound.
No kernel may reach another device: no remote copies, remote signals or barrier semaphores. Data moves between devices by JAX's collectives and lax.ppermute only.
A program may use at most 192 MiB of HBM per device.

v0:
```python
import math
import jax
import jax.numpy as jnp
from jax import lax
from jax.sharding import PartitionSpec as P

FT = 2
RT = 2
W = 32
RBANDS = 2
spatial_offsets = tuple(
    ((row_step, col_step) for row_step in (-1, 0, 1) for col_step in (-1, 0, 1))
)
frame_offsets = (-1, 0, 1)


def passed_along(shard, axis, by):
    devices = lax.axis_size(axis)
    pairs = [(i, i + by) for i in range(devices) if 0 <= i + by < devices]
    return lax.ppermute(shard, axis, pairs)


def neighbour(slab, distance):
    return passed_along(slab, "st", distance)


def circulate(data, fold, initial):
    return fold(initial, lax.all_gather(data, "ch", axis=0, tiled=True), jnp.int32(0))


def regather(data, build):
    return build(lax.all_gather(data, "ch", axis=0, tiled=True), jnp.int32(0))


def pad_rows(field):
    channels = field.shape[0]
    layered = field.reshape(channels, FT, RT * W)
    band = lax.axis_index("st") % RBANDS
    upper = neighbour(layered[:, :, (RT - 1) * W :], 1)
    lower = neighbour(layered[:, :, :W], -1)
    upper = jnp.where(band > 0, upper, jnp.zeros_like(upper))
    lower = jnp.where(band < RBANDS - 1, lower, jnp.zeros_like(lower))
    margin = jnp.zeros((channels, FT, 1), field.dtype)
    return jnp.concatenate([margin, upper, layered, lower, margin], axis=2)


def spatial_piece(padded, row_step, col_step):
    first_cell = 1 + (1 + row_step) * W + col_step
    window = lax.slice_in_dim(padded, first_cell, first_cell + RT * W, axis=2)
    column = jnp.arange(RT * W, dtype=jnp.int32) % W + col_step
    inside = (column >= 0) & (column < W)
    window = jnp.where(inside, window, jnp.zeros_like(window))
    return window.reshape(padded.shape[0], FT * RT * W)


def pad_frames(field):
    frame_cells = RT * W
    earlier = neighbour(field[:, (FT - 1) * frame_cells :], RBANDS)
    following = neighbour(field[:, :frame_cells], -RBANDS)
    return jnp.concatenate([earlier, field, following], axis=1)


def frame_piece(padded, frame_step):
    frame_cells = RT * W
    first_cell = (1 + frame_step) * frame_cells
    return lax.slice_in_dim(padded, first_cell, first_cell + FT * frame_cells, axis=1)


def contract(weights, pieces):
    running = jnp.dot(weights[0], pieces[0], preferred_element_type=jnp.float32)
    for position in range(1, len(pieces)):
        running = running + jnp.dot(
            weights[position], pieces[position], preferred_element_type=jnp.float32
        )
    return running


def outer_sums(gradient, pieces):
    contraction = (((1,), (1,)), ((), ()))
    return jnp.stack(
        [
            lax.dot_general(gradient, tap_piece, contraction, preferred_element_type=jnp.float32)
            for tap_piece in pieces
        ]
    )


def on_device(latents, spatial_weight, temporal_weight, cotangent):
    channels, tile_cells = latents.shape
    grad_scale = 1.0 / math.sqrt(tile_cells * lax.axis_size("st"))
    spatial_back, temporal_back = (
        lax.all_to_all(
            jnp.transpose(spatial_weight, (0, 2, 1)), "ch", split_axis=1, concat_axis=2, tiled=True
        ),
        lax.all_to_all(
            jnp.transpose(temporal_weight, (0, 2, 1)), "ch", split_axis=1, concat_axis=2, tiled=True
        ),
    )
    empty_sum = jnp.zeros((channels, tile_cells), jnp.float32)
    latent_pad = pad_rows(latents)
    latent_store = jnp.zeros((1,), jnp.bfloat16)

    def spatial_forward(carry, portion, offset):
        running, stored = carry
        running = contract(
            spatial_weight,
            [spatial_piece(portion, row_step, col_step) for row_step, col_step in spatial_offsets],
        )
        return (running, stored)

    spatial_sum, latent_store = circulate(latent_pad, spatial_forward, (empty_sum, latent_store))
    hidden = (latents.astype(jnp.float32) + spatial_sum).astype(jnp.bfloat16)
    hidden_pad = pad_frames(hidden)
    hidden_store = jnp.zeros((1,), jnp.bfloat16)

    def temporal_forward(carry, portion, offset):
        running, stored = carry
        running = contract(
            temporal_weight, [frame_piece(portion, frame_step) for frame_step in frame_offsets]
        )
        return (running, stored)

    temporal_sum, hidden_store = circulate(hidden_pad, temporal_forward, (empty_sum, hidden_store))
    temporal_out = (hidden.astype(jnp.float32) + temporal_sum).astype(jnp.bfloat16)
    upstream_pad = pad_frames(cotangent)

    def temporal_backward(running, portion, offset):
        return contract(
            temporal_back, [frame_piece(portion, -frame_step) for frame_step in frame_offsets]
        )

    hidden_back = circulate(upstream_pad, temporal_backward, empty_sum)

    def temporal_terms(portion, offset):
        return outer_sums(
            cotangent, [frame_piece(portion, frame_step) for frame_step in frame_offsets]
        )

    temporal_grads = regather(hidden_pad, temporal_terms)
    hidden_grad = (cotangent.astype(jnp.float32) + hidden_back).astype(jnp.bfloat16)
    grad_pad = pad_rows(hidden_grad)

    def spatial_backward(running, portion, offset):
        return contract(
            spatial_back,
            [
                spatial_piece(portion, -row_step, -col_step)
                for row_step, col_step in spatial_offsets
            ],
        )

    latent_back = circulate(grad_pad, spatial_backward, empty_sum)

    def spatial_terms(portion, offset):
        return outer_sums(
            hidden_grad,
            [spatial_piece(portion, row_step, col_step) for row_step, col_step in spatial_offsets],
        )

    spatial_grads = regather(latent_pad, spatial_terms)
    latent_grad = (hidden_grad.astype(jnp.float32) + latent_back).astype(jnp.bfloat16)
    spatial_total, temporal_total = (
        lax.psum_scatter(
            spatial_grads.astype(jnp.bfloat16), "st", scatter_dimension=2, tiled=True
        ).astype(jnp.float32),
        lax.psum_scatter(
            temporal_grads.astype(jnp.bfloat16), "st", scatter_dimension=2, tiled=True
        ).astype(jnp.float32),
    )
    return (temporal_out, latent_grad, spatial_total * grad_scale, temporal_total * grad_scale)


def solution(mesh):
    return jax.shard_map(
        on_device,
        mesh=mesh,
        in_specs=(
            P("ch", ("groups", "st")),
            P(None, "ch", None),
            P(None, "ch", None),
            P("ch", ("groups", "st")),
        ),
        out_specs=(
            P("ch", ("groups", "st")),
            P("ch", ("groups", "st")),
            P("groups", "ch", "st"),
            P("groups", "ch", "st"),
        ),
        check_vma=False,
    )
```

profile of v0, /device:TPU:0, one launch (start us, length us, event | category | flops | bytes accessed | tf_op | source)
XLA Modules:
  0.0 648.7 jit_solution(954349262117856633)
XLA Ops:
  7.2 7.7 %copy.23 = bf16[3,320,1280]{1,0,2:T(4,128)(2,1)} copy(bf16[3,320,1280]{2,1,0:T(8,128)(2,1)} %param.6) | data formatting | bytes 4915200 | tf_op args[2]
  14.9 6.3 all-to-all-start
  22.6 4.6 collective-permute-start.4
  33.0 87.4 %all_gather.16 = bf16[1280,256]{1,0:T(8,128)(2,1)S(1)} all-gather(bf16[320,256]{1,0:T(8,128)(2,1)S(1)} %pad_maximum_fusion.2), channel_id=1, replica_groups=mesh['groups'=2,'st'=4,'ch'=4] {'ch'}, dimensions={0}, use_global_device_ids=true | all-gather | bytes 819200 | tf_op jit(solution)/shard_map/all_gather | solution.py:28
  120.4 24.1 %all_gather.14 = bf16[1280,2,130]{2,1,0:T(2,128)(2,1)S(1)} all-gather(bf16[320,2,130]{2,1,0:T(2,128)(2,1)S(1)} %copy.13), channel_id=1, replica_groups=mesh['groups'=2,'st'=4,'ch'=4] {'ch'}, dimensions={0}, use_global_device_ids=true | all-gather | bytes 832000 | tf_op jit(solution)/shard_map/all_gather | solution.py:28
  144.4 4.9 copy.63
  165.1 6.9 %fusion.72 = (bf16[1280,2,64]{2,1,0:T(2,128)(2,1)S(1)}, bf16[1280,2,64]{2,1,0:T(2,128)(2,1)}, bf16[1280,2,64]{2,1,0:T(2,128)(2,1)}, bf16[1280,2,64]{2,1,0:T(2,12...) fusion(bf16[1280,2,130]{2,1,0:T(2,128)(2,1)S(1)} %all_gather.14), kind=kLoop, calls=%fused_computation.137 | loop fusion | bytes 5898240 | tf_op jit(solution)/shard_map/slice | solution.py:49
  194.4 24.4 %all_gather.17 = bf16[1280,2,130]{2,1,0:T(2,128)(2,1)S(1)} all-gather(bf16[320,2,130]{2,1,0:T(2,128)(2,1)S(1)} %copy.26), channel_id=1, replica_groups=mesh['groups'=2,'st'=4,'ch'=4] {'ch'}, dimensions={0}, use_global_device_ids=true | all-gather | bytes 832000 | tf_op jit(solution)/shard_map/all_gather | solution.py:28
  218.8 6.9 %fusion.71 = (bf16[1280,2,64]{2,1,0:T(2,128)(2,1)S(1)}, bf16[1280,2,64]{2,1,0:T(2,128)(2,1)}, bf16[1280,2,64]{2,1,0:T(2,128)(2,1)}, bf16[1280,2,64]{2,1,0:T(2,12...) fusion(bf16[1280,2,130]{2,1,0:T(2,128)(2,1)S(1)} %all_gather.17), kind=kLoop, calls=%fused_computation.136 | loop fusion | bytes 5898240 | tf_op jit(solution)/shard_map/slice | solution.py:49
  254.5 4.6 collective-permute-start.2
  261.2 17.7 %all_gather.15 = bf16[1280,256]{1,0:T(8,128)(2,1)S(1)} all-gather(bf16[320,256]{1,0:T(8,128)(2,1)S(1)} %pad_maximum_fusion.1), channel_id=1, replica_groups=mesh['groups'=2,'st'=4,'ch'=4] {'ch'}, dimensions={0}, use_global_device_ids=true | all-gather | bytes 819200 | tf_op jit(solution)/shard_map/all_gather | solution.py:28
  280.4 6.0 copy.40
  286.5 8.3 %reshape.123 = bf16[1280,960]{1,0:T(8,128)(2,1)} reshape(bf16[1280,3,320]{2,1,0:T(4,128)(2,1)} %bitcast.203) | data formatting | bytes 4915200
  294.9 20.9 %copy.28 = bf16[9,320,1280]{1,0,2:T(8,128)(2,1)} copy(bf16[9,320,1280]{2,1,0:T(8,128)(2,1)} %param.5) | data formatting | bytes 14745600 | tf_op args[1]
  327.3 20.2 %copy.38 = bf16[9,320,1280]{1,0,2:T(8,128)(2,1)} copy(bf16[9,320,1280]{2,1,0:T(8,128)(2,1)} %fusion.17) | data formatting | bytes 14745600
  347.5 18.7 %reshape.121 = bf16[1280,2880]{1,0:T(8,128)(2,1)} reshape(bf16[1280,9,320]{2,1,0:T(8,128)(2,1)} %bitcast.197) | data formatting | bytes 14745600
  366.3 14.2 %bitcast_bitcast_fusion = bf16[1280,9,320]{2,1,0:T(8,128)(2,1)} fusion(bf16[9,320,1280]{1,0,2:T(8,128)(2,1)} %copy.28), kind=kLoop, calls=%fused_computation.142 | loop fusion | bytes 14745600
  380.5 15.3 %reshape.125 = bf16[4,2,460800]{2,1,0:T(2,128)(2,1)} reshape(bf16[1280,9,320]{2,1,0:T(8,128)(2,1)} %bitcast_bitcast_fusion) | data formatting | bytes 14745600
  395.8 6.0 all-to-all-start.1
  408.6 152.6 %all-to-all-done.1 = bf16[4,2,460800]{2,1,0:T(2,128)(2,1)} async-done(((bf16[4,2,460800]{2,1,0:T(2,128)(2,1)}), bf16[4,2,460800]{2,1,0:T(2,128)(2,1)}, u32[]{:S(2)}, u32[]{:S(2)}) %all-to-all-start.1) | async-done | bytes 7372832 | tf_op jit(solution)/shard_map/all_to_all | solution.py:92
  561.2 16.0 %reshape.126 = bf16[1280,9,320]{2,1,0:T(8,128)(2,1)} reshape(bf16[4,2,460800]{2,1,0:T(2,128)(2,1)} %all-to-all-done.1) | data formatting | bytes 14745600
  577.1 12.7 %copy.62 = bf16[9,4,320,320]{3,1,2,0:T(4,128)(2,1)S(1)} copy(bf16[9,4,320,320]{3,0,2,1:T(8,128)(2,1)} %bitcast.198) | data formatting | bytes 14745600 | tf_op jit(solution)/shard_map/all_to_all | solution.py:92
  627.6 5.6 reshape.122
  633.2 6.0 copy.39
  (182 shorter events, 135.9 us)
Async XLA Ops:
  7.2 14.0 %copy-start = (bf16[320,128]{1,0:T(8,128)(2,1)S(1)}, bf16[320,128]{1,0:T(8,128)(2,1)}, u32[]{:S(2)}) copy-start(bf16[320,128]{1,0:T(8,128)(2,1)} %param.7) | copy-start | bytes 245764
  7.2 20.0 %copy-start.29 = (bf16[320,128]{1,0:T(8,128)(2,1)S(1)}, bf16[320,128]{1,0:T(8,128)(2,1)}, u32[]{:S(2)}) copy-start(bf16[320,128]{1,0:T(8,128)(2,1)} %param.4) | copy-start | bytes 245764
  14.9 129.6 %all-to-all-start = ((bf16[3,1280,320]{2,0,1:T(4,128)(2,1)}), bf16[3,1280,320]{2,0,1:T(4,128)(2,1)}, u32[]{:S(2)}, u32[]{:S(2)}) async-start(bf16[3,1280,320]{2,0,1:T(4,128)(2,1)} %bitcast.202), calls=%async_computation | async-start | bytes 7864320 | tf_op jit(solution)/shard_map/all_to_all | solution.py:95
  21.2 382.5 %reduce-scatter.9.cloned.1.call-start = ((), (), s32[]{:S(2)}) async-start(), calls=%async_computation.5 | async-start | bytes 3276800
  21.3 11.5 %collective-permute-start.5 = (bf16[320,64]{1,0:T(8,128)(2,1)S(1)}, bf16[320,64]{1,0:T(8,128)(2,1)S(1)}, u32[]{:S(2)}, u32[]{:S(2)}) collective-permute-start(bf16[320,64]{1,0:T(8,128)(2,1)S(1)} %get-tuple-element.39), channel_id=1, source_target_pairs={{8,0},{12,4},{9,1},{13,5},{10,2},{14,6},{11,3},{15,7},{24,16},{28,... | collective-permute-start | bytes 122888 | tf_op jit(solution)/shard_map/ppermute | solution.py:20
  22.6 10.2 %collective-permute-start.4 = (bf16[320,64]{1,0:T(8,128)(2,1)S(1)}, bf16[320,64]{1,0:T(8,128)(2,1)S(1)}, u32[]{:S(2)}, u32[]{:S(2)}) collective-permute-start(bf16[320,64]{1,0:T(8,128)(2,1)S(1)} %get-tuple-element.38), channel_id=1, source_target_pairs={{0,8},{4,12},{1,9},{5,13},{2,10},{6,14},{3,11},{7,15},{16,24},{20,... | collective-permute-start | bytes 122888 | tf_op jit(solution)/shard_map/ppermute | solution.py:20
  27.3 2.7 collective-permute-start
  28.6 3.1 collective-permute-start.1
  163.6 26.1 %collective-permute-start.6 = (bf16[320,2,32]{0,2,1:T(8,128)(2,1)S(1)}, bf16[320,2,32]{0,2,1:T(8,128)(2,1)S(1)}, u32[]{:S(2)}, u32[]{:S(2)}) collective-permute-start(bf16[320,2,32]{0,2,1:T(8,128)(2,1)S(1)} %get-tuple-element.35), channel_id=1, source_target_pairs={{0,4},{4,8},{8,12},{1,5},{5,9},{9,13},{2,6},{6,10},{10,14},{3,7},{... | collective-permute-start | bytes 122888 | tf_op jit(solution)/shard_map/ppermute | solution.py:20
  188.4 5.0 collective-permute-start.7
  229.0 19.7 %slice-start = ((s8[7372800]{0:T(1024)(128)(4,1)}), s8[3178496]{0:T(1024)(128)(4,1)S(1)}, s32[]{:S(2)}) async-start(s8[7372800]{0:T(1024)(128)(4,1)} %bitcast.200), calls=%async_computation.6 | async-start | bytes 6356992
  250.3 29.4 %copy-start.13 = (bf16[1280,2,64]{0,2,1:T(8,128)(2,1)}, bf16[1280,2,64]{0,2,1:T(8,128)(2,1)S(1)}, u32[]{:S(2)}) copy-start(bf16[1280,2,64]{0,2,1:T(8,128)(2,1)S(1)} %get-tuple-element.55) | copy-start | bytes 983044
  250.3 29.4 %copy-start.15 = (bf16[1280,2,64]{0,2,1:T(8,128)(2,1)}, bf16[1280,2,64]{0,2,1:T(8,128)(2,1)S(1)}, u32[]{:S(2)}) copy-start(bf16[1280,2,64]{0,2,1:T(8,128)(2,1)S(1)} %get-tuple-element.59) | copy-start | bytes 983044
  250.3 29.5 %copy-start.24 = (bf16[1280,2,64]{0,2,1:T(8,128)(2,1)}, bf16[1280,2,64]{0,2,1:T(8,128)(2,1)S(1)}, u32[]{:S(2)}) copy-start(bf16[1280,2,64]{0,2,1:T(8,128)(2,1)S(1)} %get-tuple-element.56) | copy-start | bytes 983044
  253.2 6.3 collective-permute-start.3
  254.5 6.6 %collective-permute-start.2 = (bf16[320,64]{1,0:T(8,128)(2,1)S(1)}, bf16[320,64]{1,0:T(8,128)(2,1)S(1)}, u32[]{:S(2)}, u32[]{:S(2)}) collective-permute-start(bf16[320,64]{1,0:T(8,128)(2,1)S(1)} %get-tuple-element.40), channel_id=1, source_target_pairs={{0,8},{4,12},{1,9},{5,13},{2,10},{6,14},{3,11},{7,15},{16,24},{20,... | collective-permute-start | bytes 122888 | tf_op jit(solution)/shard_map/ppermute | solution.py:20
  294.8 21.0 %copy-start.20 = (bf16[1280,2,64]{0,2,1:T(8,128)(2,1)S(1)}, bf16[1280,2,64]{0,2,1:T(8,128)(2,1)}, u32[]{:S(2)}) copy-start(bf16[1280,2,64]{0,2,1:T(8,128)(2,1)} %copy-done.19) | copy-start | bytes 983044
  294.8 22.3 %copy-start.12 = (bf16[1280,2,64]{0,2,1:T(8,128)(2,1)S(1)}, bf16[1280,2,64]{0,2,1:T(8,128)(2,1)}, u32[]{:S(2)}) copy-start(bf16[1280,2,64]{0,2,1:T(8,128)(2,1)} %copy-done.11) | copy-start | bytes 983044
  294.8 23.6 %copy-start.16 = (bf16[1280,2,64]{0,2,1:T(8,128)(2,1)S(1)}, bf16[1280,2,64]{0,2,1:T(8,128)(2,1)}, u32[]{:S(2)}) copy-start(bf16[1280,2,64]{0,2,1:T(8,128)(2,1)} %copy-done.15) | copy-start | bytes 983044
  294.8 24.9 %copy-start.6 = (bf16[1280,2,64]{0,2,1:T(8,128)(2,1)S(1)}, bf16[1280,2,64]{0,2,1:T(8,128)(2,1)}, u32[]{:S(2)}) copy-start(bf16[1280,2,64]{0,2,1:T(8,128)(2,1)} %copy-done.5) | copy-start | bytes 983044
  294.8 26.1 %copy-start.10 = (bf16[1280,2,64]{0,2,1:T(8,128)(2,1)S(1)}, bf16[1280,2,64]{0,2,1:T(8,128)(2,1)}, u32[]{:S(2)}) copy-start(bf16[1280,2,64]{0,2,1:T(8,128)(2,1)} %copy-done.9) | copy-start | bytes 983044
  294.8 27.4 %copy-start.14 = (bf16[1280,2,64]{0,2,1:T(8,128)(2,1)S(1)}, bf16[1280,2,64]{0,2,1:T(8,128)(2,1)}, u32[]{:S(2)}) copy-start(bf16[1280,2,64]{0,2,1:T(8,128)(2,1)} %copy-done.13) | copy-start | bytes 983044
  294.8 332.8 %reduce-scatter.7.cloned.1.call-start = ((), (), s32[]{:S(2)}) async-start(), calls=%async_computation.4 | async-start | bytes 9420800
  395.8 165.4 %all-to-all-start.1 = ((bf16[4,2,460800]{2,1,0:T(2,128)(2,1)}), bf16[4,2,460800]{2,1,0:T(2,128)(2,1)}, u32[]{:S(2)}, u32[]{:S(2)}) async-start(bf16[4,2,460800]{2,1,0:T(2,128)(2,1)} %reshape.125), calls=%async_computation.1 | async-start | bytes 14745600 | tf_op jit(solution)/shard_map/all_to_all | solution.py:92
  (20 other events, 148.9 us)
Sparse Core Ops, SparseCore 0:
  294.9 35.7 reduce-scatter.8
  366.4 67.7 reduce-scatter.6
where the time goes:
time: 659 us; the launch traced here: 649 us
  local copies, waits for them, and re-layouts  243 us (37%)
  waiting for transfers between devices  160 us (24%)
  blocking collectives  154 us (23%)
  matrix products  37.1 us (6%)
  starting transfers between devices  29.3 us (4%)
  between operations  15 us (2%)
  other arithmetic  10.6 us (2%)
    unnamed x96, local copies, waits for them, and re-layouts  175 us
    all_gather x4, blocking collectives, circulate(): lax.all_gather(data, 'ch', axis=0, tiled=True)  154 us
    all_to_all x1, waiting for transfers between devices, on_device(): lax.all_to_all(jnp.transpose(spatial_weight, (0, 2, 1)), 'ch', split_axis...  153 us
    squeeze x10, local copies, waits for them, and re-layouts, contract(): weights[position]  21.6 us
    dot_general x20, matrix products, contract(): jnp.dot(weights[position], pieces[position], preferred_element_type=jnp.f...  19.3 us
    ppermute x8, starting transfers between devices, passed_along(): return lax.ppermute(shard, axis, pairs)  17 us
    slice x2, local copies, waits for them, and re-layouts, spatial_piece(): window = lax.slice_in_dim(padded, first_cell, first_cell + RT * W, axis=2)  13.8 us
  transfers between devices with their start and end apart: 12, of which 5 were waited for; matrix products, arithmetic and copies ran while one was open for 31% of the time, Pallas kernels for 0%

commit v1 on v0

--- a/solution.py
+++ b/solution.py
@@ -89,8 +89,16 @@
     channels, tile_cells = latents.shape
     grad_scale = 1.0 / math.sqrt(tile_cells * lax.axis_size("st"))
     spatial_back, temporal_back = (
-        lax.all_to_all(
-            jnp.transpose(spatial_weight, (0, 2, 1)), "ch", split_axis=1, concat_axis=2, tiled=True
+        jnp.concatenate(
+            lax.all_to_all(
+                jnp.stack(
+                    jnp.split(jnp.transpose(spatial_weight, (0, 2, 1)), lax.axis_size("ch"), axis=1)
+                ),
+                "ch",
+                0,
+                0,
+            ),
+            axis=2,
         ),
         lax.all_to_all(
             jnp.transpose(temporal_weight, (0, 2, 1)), "ch", split_axis=1, concat_axis=2, tiled=True

time: 659 us -> 588 us (0.89); the launches traced: 649 us -> 586 us
  local copies, waits for them, and re-layouts: 243 us -> 149 us
  waiting for transfers between devices: 160 us -> 192 us
  matrix products: 37.1 us -> 30.3 us
    unnamed x96 -> x100, local copies, waits for them, and re-layouts: 175 us -> 109 us
    all_to_all x1, waiting for transfers between devices: 153 us -> 185 us  [on_device(): lax.all_to_all(jnp.stack(jnp.split(jnp.transpose(spatial_weight, (0, 2, 1...]
    squeeze x10 -> x2, local copies, waits for them, and re-layouts: 21.6 us -> 4.41 us  [contract(): weights[position]]
    all_to_all x1 -> x0, local copies, waits for them, and re-layouts: 12.7 us -> none  [on_device(): lax.all_to_all(jnp.transpose(spatial_weight, (0, 2, 1)), 'ch', split_axis...]
    dot_general x20, matrix products: 19.3 us -> 11.8 us  [contract(): jnp.dot(weights[position], pieces[position], preferred_element_type=jnp.f...]
  transfers between devices with their start and end apart: 12 -> 12, of which waited for: 5 -> 5; matrix products, arithmetic and copies ran while one was open for 31% -> 18% of each run, Pallas kernels for 0% -> 0%
where the time goes in v1:
time: 588 us; the launch traced here: 586 us
  waiting for transfers between devices  192 us (33%)
  blocking collectives  154 us (26%)
  local copies, waits for them, and re-layouts  149 us (25%)
  matrix products  30.3 us (5%)
  starting transfers between devices  29.8 us (5%)
  other arithmetic  16 us (3%)
  between operations  14.8 us (3%)
    all_to_all x1, waiting for transfers between devices, on_device(): lax.all_to_all(jnp.stack(jnp.split(jnp.transpose(spatial_weight, (0, 2, 1...  185 us
    all_gather x4, blocking collectives, circulate(): lax.all_gather(data, 'ch', axis=0, tiled=True)  154 us
    unnamed x100, local copies, waits for them, and re-layouts  109 us
    ppermute x8, starting transfers between devices, passed_along(): return lax.ppermute(shard, axis, pairs)  17 us
    dot_general x12, matrix products, outer_sums(): lax.dot_general(gradient, tap_piece, contraction, preferred_element_type=...  14.6 us
    slice x2, local copies, waits for them, and re-layouts, spatial_piece(): window = lax.slice_in_dim(padded, first_cell, first_cell + RT * W, axis=2)  13.8 us
    dot_general x20, matrix products, contract(): jnp.dot(weights[position], pieces[position], preferred_element_type=jnp.f...  11.8 us
  transfers between devices with their start and end apart: 12, of which 5 were waited for; matrix products, arithmetic and copies ran while one was open for 18% of the time, Pallas kernels for 0%

profile of v1, /device:TPU:0, one launch (start us, length us, event | category | flops | bytes accessed | tf_op | source)
XLA Modules:
  0.0 585.9 jit_solution(3409529734730644308)
XLA Ops:
  7.2 7.7 %copy.22 = bf16[3,320,1280]{1,0,2:T(4,128)(2,1)} copy(bf16[3,320,1280]{2,1,0:T(8,128)(2,1)} %param.6) | data formatting | bytes 4915200 | tf_op args[2]
  14.9 6.3 %all-to-all-start = ((bf16[3,1280,320]{2,0,1:T(4,128)(2,1)}), bf16[3,1280,320]{2,0,1:T(4,128)(2,1)}, u32[]{:S(2)}, u32[]{:S(2)}) async-start(bf16[3,1280,320]{2,0,1:T(4,128)(2,1)} %bitcast.205), calls=%async_computation | async-start | bytes 7864320 | tf_op jit(solution)/shard_map/all_to_all | solution.py:103
  22.6 4.6 collective-permute-start.4
  33.0 87.4 %all_gather.16 = bf16[1280,256]{1,0:T(8,128)(2,1)S(1)} all-gather(bf16[320,256]{1,0:T(8,128)(2,1)S(1)} %pad_maximum_fusion.3), channel_id=1, replica_groups=mesh['groups'=2,'st'=4,'ch'=4] {'ch'}, dimensions={0}, use_global_device_ids=true | all-gather | bytes 819200 | tf_op jit(solution)/shard_map/all_gather | solution.py:28
  120.4 24.1 %all_gather.14 = bf16[1280,2,130]{2,1,0:T(2,128)(2,1)S(1)} all-gather(bf16[320,2,130]{2,1,0:T(2,128)(2,1)S(1)} %copy.12), channel_id=1, replica_groups=mesh['groups'=2,'st'=4,'ch'=4] {'ch'}, dimensions={0}, use_global_device_ids=true | all-gather | bytes 832000 | tf_op jit(solution)/shard_map/all_gather | solution.py:28
  144.4 4.9 copy.58
  151.6 2.8 squeeze.85
  165.1 6.9 %fusion.71 = (bf16[1280,2,64]{2,1,0:T(2,128)(2,1)S(1)}, bf16[1280,2,64]{2,1,0:T(2,128)(2,1)}, bf16[1280,2,64]{2,1,0:T(2,128)(2,1)}, bf16[1280,2,64]{2,1,0:T(2,12...) fusion(bf16[1280,2,130]{2,1,0:T(2,128)(2,1)S(1)} %all_gather.14), kind=kLoop, calls=%fused_computation.140 | loop fusion | bytes 5898240 | tf_op jit(solution)/shard_map/slice | solution.py:49
  189.7 3.7 collective-permute-done.7
  194.5 24.4 %all_gather.17 = bf16[1280,2,130]{2,1,0:T(2,128)(2,1)S(1)} all-gather(bf16[320,2,130]{2,1,0:T(2,128)(2,1)S(1)} %copy.25), channel_id=1, replica_groups=mesh['groups'=2,'st'=4,'ch'=4] {'ch'}, dimensions={0}, use_global_device_ids=true | all-gather | bytes 832000 | tf_op jit(solution)/shard_map/all_gather | solution.py:28
  218.9 6.9 %fusion.70 = (bf16[1280,2,64]{2,1,0:T(2,128)(2,1)S(1)}, bf16[1280,2,64]{2,1,0:T(2,128)(2,1)}, bf16[1280,2,64]{2,1,0:T(2,128)(2,1)}, bf16[1280,2,64]{2,1,0:T(2,12...) fusion(bf16[1280,2,130]{2,1,0:T(2,128)(2,1)S(1)} %all_gather.17), kind=kLoop, calls=%fused_computation.139 | loop fusion | bytes 5898240 | tf_op jit(solution)/shard_map/slice | solution.py:49
  254.5 4.6 collective-permute-start.2
  261.3 17.7 %all_gather.15 = bf16[1280,256]{1,0:T(8,128)(2,1)S(1)} all-gather(bf16[320,256]{1,0:T(8,128)(2,1)S(1)} %pad_maximum_fusion.2), channel_id=1, replica_groups=mesh['groups'=2,'st'=4,'ch'=4] {'ch'}, dimensions={0}, use_global_device_ids=true | all-gather | bytes 819200 | tf_op jit(solution)/shard_map/all_gather | solution.py:28
  280.5 6.0 %copy.37 = bf16[3,320,1280]{1,0,2:T(4,128)(2,1)} copy(bf16[3,320,1280]{2,1,0:T(8,128)(2,1)S(1)} %pad_maximum_fusion.1) | data formatting | bytes 4915200
  286.6 8.4 %reshape.128 = bf16[1280,960]{1,0:T(8,128)(2,1)} reshape(bf16[1280,3,320]{2,1,0:T(4,128)(2,1)} %bitcast.206) | data formatting | bytes 4915200
  308.5 20.1 %copy.35 = bf16[9,320,1280]{1,0,2:T(8,128)(2,1)} copy(bf16[9,320,1280]{2,1,0:T(8,128)(2,1)} %fusion.17) | data formatting | bytes 14745600
  328.6 18.8 %reshape.126 = bf16[1280,2880]{1,0:T(8,128)(2,1)} reshape(bf16[1280,9,320]{2,1,0:T(8,128)(2,1)} %bitcast.201) | data formatting | bytes 14745600
  347.4 5.3 slice_bitcast_fusion.3
  352.8 5.4 pad_maximum_fusion
  358.1 6.4 %all-to-all-start.1 = ((bf16[4,9,320,320]{2,3,1,0:T(8,128)(2,1)}), bf16[4,9,320,320]{2,3,1,0:T(8,128)(2,1)}, u32[]{:S(2)}, u32[]{:S(2)}) async-start(bf16[4,9,320,320]{2,3,1,0:T(8,128)(2,1)} %pad_maximum_fusion), calls=%async_computation.1 | async-start | bytes 17694720 | tf_op jit(solution)/shard_map/all_to_all | solution.py:93
  371.3 184.6 %all-to-all-done.1 = bf16[4,9,320,320]{2,3,1,0:T(8,128)(2,1)} async-done(((bf16[4,9,320,320]{2,3,1,0:T(8,128)(2,1)}), bf16[4,9,320,320]{2,3,1,0:T(8,128)(2,1)}, u32[]{:S(2)}, u32[]{:S(2)}) %all-to-all-start.1) | async-done | bytes 7372832 | tf_op jit(solution)/shard_map/all_to_all | solution.py:93
  555.9 4.3 fusion.68
  565.0 5.6 reshape.127
  570.6 6.0 %copy.36 = bf16[9,320,320]{2,1,0:T(8,128)(2,1)S(1)} copy(bf16[9,320,320]{1,0,2:T(8,128)(2,1)} %bitcast.207) | data formatting | bytes 3686400
  (178 shorter events, 98.3 us)
Async XLA Ops:
  7.2 14.0 %copy-start = (bf16[320,128]{1,0:T(8,128)(2,1)S(1)}, bf16[320,128]{1,0:T(8,128)(2,1)}, u32[]{:S(2)}) copy-start(bf16[320,128]{1,0:T(8,128)(2,1)} %param.7) | copy-start | bytes 245764
  7.2 20.0 %copy-start.33 = (bf16[320,128]{1,0:T(8,128)(2,1)S(1)}, bf16[320,128]{1,0:T(8,128)(2,1)}, u32[]{:S(2)}) copy-start(bf16[320,128]{1,0:T(8,128)(2,1)} %param.4) | copy-start | bytes 245764
  14.9 129.6 %all-to-all-start = ((bf16[3,1280,320]{2,0,1:T(4,128)(2,1)}), bf16[3,1280,320]{2,0,1:T(4,128)(2,1)}, u32[]{:S(2)}, u32[]{:S(2)}) async-start(bf16[3,1280,320]{2,0,1:T(4,128)(2,1)} %bitcast.205), calls=%async_computation | async-start | bytes 7864320 | tf_op jit(solution)/shard_map/all_to_all | solution.py:103
  21.2 345.2 %reduce-scatter.9.cloned.1.call-start = ((), (), s32[]{:S(2)}) async-start(), calls=%async_computation.5 | async-start | bytes 3276800
  21.3 11.5 %collective-permute-start.5 = (bf16[320,64]{1,0:T(8,128)(2,1)S(1)}, bf16[320,64]{1,0:T(8,128)(2,1)S(1)}, u32[]{:S(2)}, u32[]{:S(2)}) collective-permute-start(bf16[320,64]{1,0:T(8,128)(2,1)S(1)} %get-tuple-element.43), channel_id=1, source_target_pairs={{8,0},{12,4},{9,1},{13,5},{10,2},{14,6},{11,3},{15,7},{24,16},{28,... | collective-permute-start | bytes 122888 | tf_op jit(solution)/shard_map/ppermute | solution.py:20
  22.6 10.2 %collective-permute-start.4 = (bf16[320,64]{1,0:T(8,128)(2,1)S(1)}, bf16[320,64]{1,0:T(8,128)(2,1)S(1)}, u32[]{:S(2)}, u32[]{:S(2)}) collective-permute-start(bf16[320,64]{1,0:T(8,128)(2,1)S(1)} %get-tuple-element.42), channel_id=1, source_target_pairs={{0,8},{4,12},{1,9},{5,13},{2,10},{6,14},{3,11},{7,15},{16,24},{20,... | collective-permute-start | bytes 122888 | tf_op jit(solution)/shard_map/ppermute | solution.py:20
  27.3 2.7 collective-permute-start
  28.6 3.1 collective-permute-start.1
  163.6 26.0 %collective-permute-start.6 = (bf16[320,2,32]{0,2,1:T(8,128)(2,1)S(1)}, bf16[320,2,32]{0,2,1:T(8,128)(2,1)S(1)}, u32[]{:S(2)}, u32[]{:S(2)}) collective-permute-start(bf16[320,2,32]{0,2,1:T(8,128)(2,1)S(1)} %get-tuple-element.39), channel_id=1, source_target_pairs={{0,4},{4,8},{8,12},{1,5},{5,9},{9,13},{2,6},{6,10},{10,14},{3,7},{... | collective-permute-start | bytes 122888 | tf_op jit(solution)/shard_map/ppermute | solution.py:20
  188.4 5.0 collective-permute-start.7
  229.1 19.8 %slice-start = ((s8[7372800]{0:T(1024)(128)(4,1)}), s8[3178496]{0:T(1024)(128)(4,1)S(1)}, s32[]{:S(2)}) async-start(s8[7372800]{0:T(1024)(128)(4,1)} %bitcast.203), calls=%async_computation.6 | async-start | bytes 6356992
  250.4 29.4 %copy-start.11 = (bf16[1280,2,64]{0,2,1:T(8,128)(2,1)}, bf16[1280,2,64]{0,2,1:T(8,128)(2,1)S(1)}, u32[]{:S(2)}) copy-start(bf16[1280,2,64]{0,2,1:T(8,128)(2,1)S(1)} %get-tuple-element.59) | copy-start | bytes 983044
  250.4 29.4 %copy-start.13 = (bf16[1280,2,64]{0,2,1:T(8,128)(2,1)}, bf16[1280,2,64]{0,2,1:T(8,128)(2,1)S(1)}, u32[]{:S(2)}) copy-start(bf16[1280,2,64]{0,2,1:T(8,128)(2,1)S(1)} %get-tuple-element.63) | copy-start | bytes 983044
  250.4 29.4 %copy-start.29 = (bf16[1280,2,64]{0,2,1:T(8,128)(2,1)}, bf16[1280,2,64]{0,2,1:T(8,128)(2,1)S(1)}, u32[]{:S(2)}) copy-start(bf16[1280,2,64]{0,2,1:T(8,128)(2,1)S(1)} %get-tuple-element.60) | copy-start | bytes 983044
  253.2 6.3 %collective-permute-start.3 = (bf16[320,64]{1,0:T(8,128)(2,1)S(1)}, bf16[320,64]{1,0:T(8,128)(2,1)S(1)}, u32[]{:S(2)}, u32[]{:S(2)}) collective-permute-start(bf16[320,64]{1,0:T(8,128)(2,1)S(1)} %get-tuple-element.45), channel_id=1, source_target_pairs={{8,0},{12,4},{9,1},{13,5},{10,2},{14,6},{11,3},{15,7},{24,16},{28,... | collective-permute-start | bytes 122888 | tf_op jit(solution)/shard_map/ppermute | solution.py:20
  254.5 6.6 %collective-permute-start.2 = (bf16[320,64]{1,0:T(8,128)(2,1)S(1)}, bf16[320,64]{1,0:T(8,128)(2,1)S(1)}, u32[]{:S(2)}, u32[]{:S(2)}) collective-permute-start(bf16[320,64]{1,0:T(8,128)(2,1)S(1)} %get-tuple-element.44), channel_id=1, source_target_pairs={{0,8},{4,12},{1,9},{5,13},{2,10},{6,14},{3,11},{7,15},{16,24},{20,... | collective-permute-start | bytes 122888 | tf_op jit(solution)/shard_map/ppermute | solution.py:20
  286.5 12.0 %copy-start.14 = (bf16[1280,2,64]{0,2,1:T(8,128)(2,1)S(1)}, bf16[1280,2,64]{0,2,1:T(8,128)(2,1)}, u32[]{:S(2)}) copy-start(bf16[1280,2,64]{0,2,1:T(8,128)(2,1)} %copy-done.13) | copy-start | bytes 983044
  286.5 13.3 %copy-start.4 = (bf16[1280,2,64]{0,2,1:T(8,128)(2,1)S(1)}, bf16[1280,2,64]{0,2,1:T(8,128)(2,1)}, u32[]{:S(2)}) copy-start(bf16[1280,2,64]{0,2,1:T(8,128)(2,1)} %copy-done.3) | copy-start | bytes 983044
  286.5 14.6 %copy-start.8 = (bf16[1280,2,64]{0,2,1:T(8,128)(2,1)S(1)}, bf16[1280,2,64]{0,2,1:T(8,128)(2,1)}, u32[]{:S(2)}) copy-start(bf16[1280,2,64]{0,2,1:T(8,128)(2,1)} %copy-done.7) | copy-start | bytes 983044
  286.5 15.9 %copy-start.12 = (bf16[1280,2,64]{0,2,1:T(8,128)(2,1)S(1)}, bf16[1280,2,64]{0,2,1:T(8,128)(2,1)}, u32[]{:S(2)}) copy-start(bf16[1280,2,64]{0,2,1:T(8,128)(2,1)} %copy-done.11) | copy-start | bytes 983044
  286.5 17.1 %copy-start.2 = (bf16[1280,2,64]{0,2,1:T(8,128)(2,1)S(1)}, bf16[1280,2,64]{0,2,1:T(8,128)(2,1)}, u32[]{:S(2)}) copy-start(bf16[1280,2,64]{0,2,1:T(8,128)(2,1)} %copy-done.1) | copy-start | bytes 983044
  286.6 18.4 %copy-start.6 = (bf16[1280,2,64]{0,2,1:T(8,128)(2,1)S(1)}, bf16[1280,2,64]{0,2,1:T(8,128)(2,1)}, u32[]{:S(2)}) copy-start(bf16[1280,2,64]{0,2,1:T(8,128)(2,1)} %copy-done.5) | copy-start | bytes 983044
  295.0 270.0 %reduce-scatter.7.cloned.1.call-start = ((), (), s32[]{:S(2)}) async-start(), calls=%async_computation.4 | async-start | bytes 9420800
  358.1 197.8 %all-to-all-start.1 = ((bf16[4,9,320,320]{2,3,1,0:T(8,128)(2,1)}), bf16[4,9,320,320]{2,3,1,0:T(8,128)(2,1)}, u32[]{:S(2)}, u32[]{:S(2)}) async-start(bf16[4,9,320,320]{2,3,1,0:T(8,128)(2,1)} %pad_maximum_fusion), calls=%async_computation.1 | async-start | bytes 17694720 | tf_op jit(solution)/shard_map/all_to_all | solution.py:93
  (24 other events, 139.6 us)
Sparse Core Ops, SparseCore 0:
  295.1 35.8 reduce-scatter.8
  347.5 67.9 reduce-scatter.6
